TPU v7x, 128 devices: a whole 4x4x4 slice. The times are simulated.
128 devices in a mesh: ray: 16 (over x, z), tile: 8 (over y, core).
Axes of the slice: x: 4, y: 4, z: 4, core: 2. Of those that a mesh axis runs over, the one named last changes fastest.
Arguments:
- data: float32 [64, 262144], P(None, ('ray', 'tile')), may hold values from -6 to 6
- sensitivity: bfloat16 [4096, 256, 512], P(('ray', 'tile')), may hold values from -0.25 to 0.25
- block_tiles: int32 [128, 8, 4], P(('ray', 'tile')), may hold values from 0 to 47
- block_bundles: int32 [128, 8, 4], P(('ray', 'tile')), may hold values from 0 to 7
Outputs:
- solution: float32 [64, 196608], P(None, 'tile')
- residual: float32 [64, 262144], P(None, ('ray', 'tile'))
Inputs may be any that keep to these rules, and one draw needn't show every extreme that they name: `block_tiles`: position of the block's tile among the 48 tiles of the owner given by the second index. `block_bundles`: the block's ray bundle among the device's 8 bundles.
All inputs are finite; a program needn't handle non-finite values.
Results may differ from a plain program's by a relative error of at most 0.004.
The roundings to bfloat16 on the way count: a program that leaves them out, or rounds other values in their place, can miss the bound.
Values may be sent and summed in bfloat16 or wider, within the bound.
A program may use at most 128 MiB of HBM per device.

v0:
```python
import jax
import jax.numpy as jnp
from jax import lax
from jax.sharding import PartitionSpec as P

RB = 256
CB = 512
ITERS = 2
BUND_DEV = 8
TILE_DEV = 48
eps_norm = 1e-06


def per_device(data, sensitivity, block_tiles, block_bundles):
    columns = data.shape[0]
    bundles = block_bundles.reshape(-1)
    requests = lax.all_to_all(block_tiles, "tile", split_axis=1, concat_axis=1, tiled=True).reshape(
        -1
    )
    bundle_onehot = (bundles[:, None] == jnp.arange(BUND_DEV, dtype=jnp.int32)[None, :]).astype(
        jnp.float32
    )
    owner_onehot = (requests[:, None] == jnp.arange(TILE_DEV, dtype=jnp.int32)[None, :]).astype(
        jnp.bfloat16
    )

    def fetch(field_bf):
        owned = field_bf.reshape(columns, TILE_DEV, CB)
        outgoing = jnp.take(owned, requests, axis=1)
        tiles = lax.all_to_all(outgoing, "tile", split_axis=1, concat_axis=1, tiled=True)
        return tiles

    def forward(field_bf):
        tiles = fetch(field_bf)
        partial_value = jnp.einsum(
            "cnk,nrk->ncr", tiles, sensitivity, preferred_element_type=jnp.float32
        )
        summed = jnp.einsum(
            "ncr,nb->cbr", partial_value, bundle_onehot, precision=lax.Precision.HIGHEST
        )
        return summed.reshape(columns, BUND_DEV * RB)

    def adjoint(rays_bf):
        picked = jnp.take(rays_bf.reshape(columns, BUND_DEV, RB), bundles, axis=1)
        terms = jnp.einsum(
            "cnr,nrk->cnk", picked, sensitivity, preferred_element_type=jnp.float32
        ).astype(jnp.bfloat16)
        arrived = lax.all_to_all(terms, "tile", split_axis=1, concat_axis=1, tiled=True)
        owned = jnp.einsum(
            "cnk,nt->ctk", arrived, owner_onehot, preferred_element_type=jnp.float32
        ).reshape(columns, TILE_DEV * CB)
        total = lax.psum(owned, "ray")
        return total

    def cell_norm(field):
        local = jnp.sum(field * field, axis=1)
        total = lax.psum(local, "tile")
        return jnp.sqrt(total + eps_norm)

    def ray_norm(rays):
        total = lax.psum(jnp.sum(rays * rays, axis=1), ("ray", "tile"))
        return jnp.sqrt(total + eps_norm)

    beta_now = ray_norm(data)
    rays_dir = data / beta_now[:, None]
    model_dir = adjoint(rays_dir.astype(jnp.bfloat16))
    alpha_now = cell_norm(model_dir)
    model_dir = model_dir / alpha_now[:, None]
    search = model_dir
    solution = jnp.zeros_like(model_dir)
    phi_bar = beta_now
    rho_bar = alpha_now
    for step in range(ITERS):
        rounded = model_dir.astype(jnp.bfloat16)
        rays_dir = forward(rounded) - alpha_now[:, None] * rays_dir
        beta_now = ray_norm(rays_dir)
        rays_dir = rays_dir / beta_now[:, None]
        rho_now = jnp.sqrt(rho_bar * rho_bar + beta_now * beta_now)
        cosine = rho_bar / rho_now
        sine_part = beta_now / rho_now
        phi_now = cosine * phi_bar
        phi_bar = sine_part * phi_bar
        solution = solution + (phi_now / rho_now)[:, None] * search
        if step + 1 < ITERS:
            model_dir = adjoint(rays_dir.astype(jnp.bfloat16)) - beta_now[:, None] * model_dir
            alpha_now = cell_norm(model_dir)
            model_dir = model_dir / alpha_now[:, None]
            theta_now = sine_part * alpha_now
            rho_bar = -cosine * alpha_now
            search = model_dir - (theta_now / rho_now)[:, None] * search
    residual = data - forward(solution.astype(jnp.bfloat16))
    return (solution, residual)


def solution(mesh):
    return jax.shard_map(
        per_device,
        mesh=mesh,
        in_specs=(
            P(None, ("ray", "tile")),
            P(("ray", "tile"), None, None),
            P(("ray", "tile"), None, None),
            P(("ray", "tile"), None, None),
        ),
        out_specs=(P(None, "tile"), P(None, ("ray", "tile"))),
        check_vma=False,
    )
```

profile of v0, /device:TPU:1, one launch (start us, length us, event | category | flops | bytes accessed | tf_op | source)
XLA Modules:
  0.0 731.6 jit_solution(17410393598439722855)
XLA Ops:
  7.2 1.3 copy.22
  8.5 6.0 all-to-all-start
  14.5 0.8 copy.23
  15.3 1.2 multiply_reduce_fusion.4
  16.5 67.7 %psum.49 = f32[64]{0:T(128)S(1)} all-reduce(f32[64]{0:T(128)S(1)} %multiply_reduce_fusion.4), channel_id=1, replica_groups=mesh['ray'=16,'tile'=8] {'ray','tile'}, use_global_device_ids=true, to_apply=%region_1.0 | all-reduce | flops 64 | bytes 512 | tf_op jit(solution)/shard_map/psum | solution.py:61
  84.3 1.1 fusion.19
  85.5 0.6 gather_fusion
  86.1 6.3 convert_bitcast_fusion.1
  92.4 4.4 all-to-all-start.1
  96.8 0.5 broadcast.102
  97.3 0.7 reduce.3
  98.1 25.1 %all-to-all-done.1 = bf16[64,32,512]{2,0,1:T(8,128)(2,1)S(1)} async-done(((bf16[64,32,512]{2,0,1:T(8,128)(2,1)}), bf16[64,32,512]{2,0,1:T(8,128)(2,1)S(1)}, u32[]{:S(2)}, u32[]{:S(2)}) %all-to-all-start.1) | async-done | bytes 2097184 | tf_op jit(solution)/shard_map/all_to_all | solution.py:48
  123.1 1.7 fusion.8
  124.9 6.3 copy.39
  131.3 119.1 %all-reduce.3.cloned.1.call-done = f32[64,24576]{1,0:T(8,128)} async-done(((f32[64,24576]{1,0:T(8,128)}), f32[64,24576]{1,0:T(8,128)}) %all-reduce.3.cloned.1.call-update) | async-done | bytes 6291472 | tf_op jit(solution)/shard_map/psum | solution.py:52
  250.4 3.3 multiply_reduce_fusion.1
  253.7 12.4 %psum.51 = f32[64]{0:T(128)S(1)} all-reduce(f32[64]{0:T(128)S(1)} %multiply_reduce_fusion.1), channel_id=1, replica_groups=mesh['ray'=16,'tile'=8] {'tile'}, use_global_device_ids=true, to_apply=%region_4.6 | all-reduce | flops 64 | bytes 512 | tf_op jit(solution)/shard_map/psum | solution.py:57
  266.1 3.2 fusion.37
  269.4 0.4 copy.61
  269.8 2.0 gather_fusion.1
  271.8 1.8 select_bitcast_fusion.2
  273.7 31.7 %all_to_all.30 = bf16[64,32,512]{2,0,1:T(8,128)(2,1)S(1)} all-to-all(bf16[64,32,512]{2,0,1:T(8,128)(2,1)S(1)} %select_bitcast_fusion.2), channel_id=1, replica_groups=mesh['ray'=16,'tile'=8] {'tile'}, dimensions={1} | all-to-all | bytes 4194304 | tf_op jit(solution)/shard_map/all_to_all | solution.py:30
  305.4 6.0 fusion.41
  311.5 2.0 fusion.6
  313.9 64.5 %psum.52 = f32[64]{0:T(128)S(1)} all-reduce(f32[64]{0:T(128)S(1)} %get-tuple-element.11), channel_id=1, replica_groups=mesh['ray'=16,'tile'=8] {'ray','tile'}, use_global_device_ids=true, to_apply=%region_6.0 | all-reduce | flops 64 | bytes 512 | tf_op jit(solution)/shard_map/psum | solution.py:61
  378.6 0.6 gather_fusion.2
  379.2 5.0 convert_bitcast_fusion
  384.2 30.1 %all_to_all.31 = bf16[64,32,512]{2,0,1:T(8,128)(2,1)S(1)} all-to-all(bf16[64,32,512]{2,0,1:T(8,128)(2,1)S(1)} %convert_bitcast_fusion), channel_id=1, replica_groups=mesh['ray'=16,'tile'=8] {'tile'}, dimensions={1} | all-to-all | bytes 4194304 | tf_op jit(solution)/shard_map/all_to_all | solution.py:48
  414.3 1.7 fusion.4
  416.0 6.3 copy.41
  422.3 118.9 %all-reduce.5.cloned.1.call-done = f32[64,24576]{1,0:T(8,128)} async-done(((f32[64,24576]{1,0:T(8,128)}), f32[64,24576]{1,0:T(8,128)}) %all-reduce.5.cloned.1.call-update) | async-done | bytes 6291472 | tf_op jit(solution)/shard_map/psum | solution.py:52
  541.2 5.8 multiply_reduce_fusion
  547.0 12.4 %psum.54 = f32[64]{0:T(128)S(1)} all-reduce(f32[64]{0:T(128)S(1)} %multiply_reduce_fusion), channel_id=1, replica_groups=mesh['ray'=16,'tile'=8] {'tile'}, use_global_device_ids=true, to_apply=%region_9.12 | all-reduce | flops 64 | bytes 512 | tf_op jit(solution)/shard_map/psum | solution.py:57
  559.4 5.2 fusion.10
  564.6 0.4 copy.60
  565.1 2.0 gather_fusion.3
  567.1 1.8 select_bitcast_fusion.1
  568.9 31.7 %all_to_all.32 = bf16[64,32,512]{2,0,1:T(8,128)(2,1)S(1)} all-to-all(bf16[64,32,512]{2,0,1:T(8,128)(2,1)S(1)} %select_bitcast_fusion.1), channel_id=1, replica_groups=mesh['ray'=16,'tile'=8] {'tile'}, dimensions={1} | all-to-all | bytes 4194304 | tf_op jit(solution)/shard_map/all_to_all | solution.py:30
  600.7 6.0 fusion.42
  606.7 2.0 fusion.2
  609.1 64.8 %psum.55 = f32[64]{0:T(128)S(1)} all-reduce(f32[64]{0:T(128)S(1)} %multiply_reduce_fusion.2), channel_id=1, replica_groups=mesh['ray'=16,'tile'=8] {'ray','tile'}, use_global_device_ids=true, to_apply=%region_11.14 | all-reduce | flops 64 | bytes 512 | tf_op jit(solution)/shard_map/psum | solution.py:61
  673.9 7.4 %fusion.38 = (bf16[64,24576]{1,0:T(8,128)(2,1)S(1)}, f32[64,24576]{1,0:T(8,128)}) fusion(f32[64]{0:T(128)S(1)} %multiply_divide_fusion, f32[64]{0:T(128)S(1)} %add_sqrt_fusion, f32[64,24576]{1,0:T(8,128)} %all-reduce.5.cloned.1.call-done, f32[64]{0:T(128)S(1)} %get-tuple-element.13, f32[64]{0:T(128)S(1)} %get-tuple-element.9, ...), kind=kLoop, calls=%fused_computation.76 | loop fusion | flops 15728640 | bytes 22021632 | tf_op jit(solution)/shard_map/convert_element_type | solution.py:91
  681.7 2.0 gather_fusion.4
  683.7 1.8 select_bitcast_fusion
  685.6 30.1 %all_to_all.33 = bf16[64,32,512]{2,0,1:T(8,128)(2,1)S(1)} all-to-all(bf16[64,32,512]{2,0,1:T(8,128)(2,1)S(1)} %select_bitcast_fusion), channel_id=1, replica_groups=mesh['ray'=16,'tile'=8] {'tile'}, dimensions={1} | all-to-all | bytes 4194304 | tf_op jit(solution)/shard_map/all_to_all | solution.py:30
  715.7 6.0 fusion.43
  721.8 2.0 fusion
  723.9 0.9 sub.19
  (36 shorter events, 1.9 us)
Async XLA Ops:
  8.5 83.9 %all-to-all-start = ((s32[1,8,4]{2,0,1:T(1,128)}), s32[1,8,4]{2,0,1:T(1,128)S(1)}, u32[]{:S(2)}, u32[]{:S(2)}) async-start(s32[1,8,4]{2,0,1:T(1,128)} %copy.22), calls=%async_computation | async-start | bytes 8192 | tf_op jit(solution)/shard_map/all_to_all | solution.py:17
  92.4 30.8 %all-to-all-start.1 = ((bf16[64,32,512]{2,0,1:T(8,128)(2,1)}), bf16[64,32,512]{2,0,1:T(8,128)(2,1)S(1)}, u32[]{:S(2)}, u32[]{:S(2)}) async-start(bf16[64,32,512]{2,0,1:T(8,128)(2,1)} %convert_bitcast_fusion.1), calls=%async_computation.1 | async-start | bytes 4194304 | tf_op jit(solution)/shard_map/all_to_all | solution.py:48
  96.8 153.6 %all-reduce.3.cloned.1.call-start = ((), (), s32[]{:S(2)}) async-start(), calls=%async_computation.6 | async-start | bytes 12582912 | tf_op jit(solution)/shard_map/psum | solution.py:52
  131.2 410.0 %all-reduce.5.cloned.1.call-start = ((), (), s32[]{:S(2)}) async-start(), calls=%async_computation.7 | async-start | bytes 12582912 | tf_op jit(solution)/shard_map/psum | solution.py:52
  311.4 2.1 copy-start
  313.9 64.7 %copy-start.2 = (f32[64,2048]{1,0:T(8,128)}, f32[64,2048]{1,0:T(8,128)S(1)}, u32[]{:S(2)}) copy-start(f32[64,2048]{1,0:T(8,128)S(1)} %get-tuple-element.12) | copy-start | bytes 1572868
  606.7 2.1 copy-start.3
  721.7 2.1 copy-start.1
Sparse Core Ops, SparseCore 0:
  131.3 119.0 all-reduce.2
  422.4 118.6 all-reduce.4
where the time goes:
time: 733 us; the launch traced here: 732 us
  blocking collectives  346 us (47%)
  waiting for transfers between devices  263 us (36%)
  matrix products  38.8 us (5%)
  other arithmetic  35 us (5%)
  local copies, waits for them, and re-layouts  24.4 us (3%)
  between operations  14.3 us (2%)
  starting transfers between devices  10.4 us (1%)
    psum x2, waiting for transfers between devices, adjoint(): total = lax.psum(owned, 'ray')  238 us
    psum x3, blocking collectives, ray_norm(): total = lax.psum(jnp.sum(rays * rays, axis=1), ('ray', 'tile'))  197 us
    all_to_all x3, blocking collectives, fetch(): lax.all_to_all(outgoing, 'tile', split_axis=1, concat_axis=1, tiled=True)  93.6 us
    all_to_all x1, blocking collectives, adjoint(): lax.all_to_all(terms, 'tile', split_axis=1, concat_axis=1, tiled=True)  30.1 us
    all_to_all x1, waiting for transfers between devices, adjoint(): lax.all_to_all(terms, 'tile', split_axis=1, concat_axis=1, tiled=True)  25.1 us
    psum x2, blocking collectives, cell_norm(): total = lax.psum(local, 'tile')  24.9 us
    dot_general x3, matrix products, forward(): jnp.einsum('cnk,nrk->ncr', tiles, sensitivity, preferred_element_type=jnp...  18.1 us
    unnamed x15, local copies, waits for them, and re-layouts  15.1 us
  transfers between devices with their start and end apart: 4, of which 3 were waited for; matrix products, arithmetic and copies ran while one was open for 2% of the time, Pallas kernels for 0%

commit v1 on v0

--- a/solution.py
+++ b/solution.py
@@ -49,7 +49,7 @@
         owned = jnp.einsum(
             "cnk,nt->ctk", arrived, owner_onehot, preferred_element_type=jnp.float32
         ).reshape(columns, TILE_DEV * CB)
-        total = lax.psum(owned, "ray")
+        total = jnp.sum(lax.all_gather(owned, "ray"), axis=0)
         return total
 
     def cell_norm(field):

time: 733 us -> 1640 us (2.24)
  waiting for transfers between devices: 263 us -> 1120 us
  other arithmetic: 35 us -> 110 us
  blocking collectives: 346 us -> 316 us
    all_gather x0 -> x2, waiting for transfers between devices: none -> 1070 us  [adjoint(): total = jnp.sum(lax.all_gather(owned, 'ray'), axis=0)]
    psum x2 -> x0, waiting for transfers between devices: 238 us -> none  [adjoint(): total = lax.psum(owned, 'ray')]
    reduce_sum x0 -> x2, other arithmetic: none -> 67.1 us  [adjoint(): total = jnp.sum(lax.all_gather(owned, 'ray'), axis=0)]
    all_to_all x3 -> x2, blocking collectives: 93.6 us -> 63.5 us  [fetch(): lax.all_to_all(outgoing, 'tile', split_axis=1, concat_axis=1, tiled=True)]
    all_to_all x0 -> x1, waiting for transfers between devices: none -> 19 us  [fetch(): lax.all_to_all(outgoing, 'tile', split_axis=1, concat_axis=1, tiled=True)]
  transfers between devices with their start and end apart: 4 -> 5, of which waited for: 3 -> 4; matrix products, arithmetic and copies ran while one was open for 2% -> 1% of each run, Pallas kernels for 0% -> 0%
where the time goes in v1:
time: 1640 us
  waiting for transfers between devices  1120 us (68%)
  blocking collectives  316 us (19%)
  other arithmetic  110 us (7%)
  matrix products  44.2 us (3%)
  local copies, waits for them, and re-layouts  23 us (1%)
    all_gather x2, waiting for transfers between devices, adjoint(): total = jnp.sum(lax.all_gather(owned, 'ray'), axis=0)  1070 us
    psum x3, blocking collectives, ray_norm(): total = lax.psum(jnp.sum(rays * rays, axis=1), ('ray', 'tile'))  197 us
    reduce_sum x2, other arithmetic, adjoint(): total = jnp.sum(lax.all_gather(owned, 'ray'), axis=0)  67.1 us
    all_to_all x2, blocking collectives, fetch(): lax.all_to_all(outgoing, 'tile', split_axis=1, concat_axis=1, tiled=True)  63.5 us
  transfers between devices with their start and end apart: 5, of which 4 were waited for; matrix products, arithmetic and copies ran while one was open for 1% of the time, Pallas kernels for 0%

profile of v1, /device:TPU:1, one launch (start us, length us, event | category | flops | bytes accessed | tf_op | source)
XLA Modules:
  0.0 1638.3 jit_solution(7632157956531530285)
XLA Ops:
  7.2 1.3 copy.21
  8.5 6.0 all-to-all-start
  14.5 0.8 copy.22
  15.3 1.2 multiply_reduce_fusion.4
  16.5 67.7 %psum.35 = f32[64]{0:T(128)S(1)} all-reduce(f32[64]{0:T(128)S(1)} %multiply_reduce_fusion.4), channel_id=1, replica_groups=mesh['ray'=16,'tile'=8] {'ray','tile'}, use_global_device_ids=true, to_apply=%region_1.0 | all-reduce | flops 64 | bytes 512 | tf_op jit(solution)/shard_map/psum | solution.py:61
  84.3 1.1 fusion.17
  85.4 0.6 gather_fusion
  86.1 6.3 convert_bitcast_fusion.1
  92.4 4.4 all-to-all-start.1
  97.3 0.7 reduce.3
  98.0 25.1 %all-to-all-done.1 = bf16[64,32,512]{2,0,1:T(8,128)(2,1)S(1)} async-done(((bf16[64,32,512]{2,0,1:T(8,128)(2,1)}), bf16[64,32,512]{2,0,1:T(8,128)(2,1)S(1)}, u32[]{:S(2)}, u32[]{:S(2)}) %all-to-all-start.1) | async-done | bytes 2097184 | tf_op jit(solution)/shard_map/all_to_all | solution.py:48
  123.1 4.4 convolution_bitcast_fusion.1
  127.6 6.2 all_gather_reshape.6
  133.9 536.2 %all-gather.3.cloned.1.call-done = f32[16,64,24576]{2,1,0:T(8,128)} async-done(((f32[1,64,24576]{2,1,0:T(8,128)}), f32[16,64,24576]{2,1,0:T(8,128)}) %all-gather.3.cloned.1.call-update) | async-done | bytes 100663312 | tf_op jit(solution)/shard_map/all_gather | solution.py:52
  670.1 33.6 %reduce_sum.68 = f32[64,24576]{1,0:T(8,128)} reduce(f32[16,64,24576]{2,1,0:T(8,128)} %all-gather.3.cloned.1.call-done, f32[]{:T(128)} %constant.18.clone.1), dimensions={0}, to_apply=%region_2.0 | reduce | flops 23592960 | bytes 106954752 | tf_op jit(solution)/shard_map/reduce_sum | solution.py:52
  703.7 3.3 multiply_reduce_fusion.1
  707.0 12.4 psum.36
  719.5 3.7 fusion.36
  723.2 2.0 gather_fusion.1
  725.3 1.8 select_bitcast_fusion.2
  727.1 31.7 %all_to_all.30 = bf16[64,32,512]{2,0,1:T(8,128)(2,1)S(1)} all-to-all(bf16[64,32,512]{2,0,1:T(8,128)(2,1)S(1)} %select_bitcast_fusion.2), channel_id=1, replica_groups=mesh['ray'=16,'tile'=8] {'tile'}, dimensions={1} | all-to-all | bytes 4194304 | tf_op jit(solution)/shard_map/all_to_all | solution.py:30
  758.8 6.1 fusion.39
  764.9 2.0 fusion.6
  767.4 64.7 %psum.37 = f32[64]{0:T(128)S(1)} all-reduce(f32[64]{0:T(128)S(1)} %get-tuple-element.9), channel_id=1, replica_groups=mesh['ray'=16,'tile'=8] {'ray','tile'}, use_global_device_ids=true, to_apply=%region_6.0 | all-reduce | flops 64 | bytes 512 | tf_op jit(solution)/shard_map/psum | solution.py:61
  832.9 5.0 convert_bitcast_fusion
  837.9 30.1 %all_to_all.31 = bf16[64,32,512]{2,0,1:T(8,128)(2,1)S(1)} all-to-all(bf16[64,32,512]{2,0,1:T(8,128)(2,1)S(1)} %convert_bitcast_fusion), channel_id=1, replica_groups=mesh['ray'=16,'tile'=8] {'tile'}, dimensions={1} | all-to-all | bytes 4194304 | tf_op jit(solution)/shard_map/all_to_all | solution.py:48
  868.0 4.4 convolution_bitcast_fusion
  872.4 6.2 all_gather_reshape.7
  878.6 535.9 %all-gather.5.cloned.1.call-done = f32[16,64,24576]{2,1,0:T(8,128)} async-done(((f32[1,64,24576]{2,1,0:T(8,128)}), f32[16,64,24576]{2,1,0:T(8,128)}) %all-gather.5.cloned.1.call-update) | async-done | bytes 100663312 | tf_op jit(solution)/shard_map/all_gather | solution.py:52
  1414.5 33.5 %reduce_sum.72 = f32[64,24576]{1,0:T(8,128)} reduce(f32[16,64,24576]{2,1,0:T(8,128)} %all-gather.5.cloned.1.call-done, f32[]{:T(128)} %constant.18.clone.1), dimensions={0}, to_apply=%region_7.10 | reduce | flops 23592960 | bytes 106954752 | tf_op jit(solution)/shard_map/reduce_sum | solution.py:52
  1448.0 5.8 multiply_reduce_fusion
  1453.8 12.4 psum.38
  1466.3 5.6 fusion.35
  1471.8 2.0 gather_fusion.3
  1473.9 1.8 select_bitcast_fusion.1
  1475.7 31.7 %all_to_all.32 = bf16[64,32,512]{2,0,1:T(8,128)(2,1)S(1)} all-to-all(bf16[64,32,512]{2,0,1:T(8,128)(2,1)S(1)} %select_bitcast_fusion.1), channel_id=1, replica_groups=mesh['ray'=16,'tile'=8] {'tile'}, dimensions={1} | all-to-all | bytes 4194304 | tf_op jit(solution)/shard_map/all_to_all | solution.py:30
  1507.4 6.1 fusion.40
  1513.5 2.0 fusion.3
  1516.0 64.7 %psum.39 = f32[64]{0:T(128)S(1)} all-reduce(f32[64]{0:T(128)S(1)} %multiply_reduce_fusion.2), channel_id=1, replica_groups=mesh['ray'=16,'tile'=8] {'ray','tile'}, use_global_device_ids=true, to_apply=%region_11.14 | all-reduce | flops 64 | bytes 512 | tf_op jit(solution)/shard_map/psum | solution.py:61
  1580.7 5.8 add_convert_fusion
  1586.5 2.0 gather_fusion.4
  1588.5 3.2 select_bitcast_fusion
  1591.7 4.3 all-to-all-start.5
  1596.1 7.3 multiply_add_fusion
  1603.4 19.0 %all-to-all-done.5 = bf16[64,32,512]{2,0,1:T(8,128)(2,1)S(1)} async-done(((bf16[64,32,512]{2,0,1:T(8,128)(2,1)}), bf16[64,32,512]{2,0,1:T(8,128)(2,1)S(1)}, u32[]{:S(2)}, u32[]{:S(2)}) %all-to-all-start.5) | async-done | bytes 2097184 | tf_op jit(solution)/shard_map/all_to_all | solution.py:30
  1622.4 6.0 fusion.41
  1628.4 2.0 fusion.1
  1630.6 0.9 sub.28
  (37 shorter events, 2.7 us)
Async XLA Ops:
  8.5 83.9 %all-to-all-start = ((s32[1,8,4]{2,0,1:T(1,128)}), s32[1,8,4]{2,0,1:T(1,128)S(1)}, u32[]{:S(2)}, u32[]{:S(2)}) async-start(s32[1,8,4]{2,0,1:T(1,128)} %copy.21), calls=%async_computation | async-start | bytes 8192 | tf_op jit(solution)/shard_map/all_to_all | solution.py:17
  92.4 30.8 %all-to-all-start.1 = ((bf16[64,32,512]{2,0,1:T(8,128)(2,1)}), bf16[64,32,512]{2,0,1:T(8,128)(2,1)S(1)}, u32[]{:S(2)}, u32[]{:S(2)}) async-start(bf16[64,32,512]{2,0,1:T(8,128)(2,1)} %convert_bitcast_fusion.1), calls=%async_computation.1 | async-start | bytes 4194304 | tf_op jit(solution)/shard_map/all_to_all | solution.py:48
  96.8 573.3 %all-gather.3.cloned.1.call-start = ((), (), s32[]{:S(2)}) async-start(), calls=%async_computation.6 | async-start | bytes 106954752 | tf_op jit(solution)/shard_map/all_gather | solution.py:52
  133.8 1280.7 %all-gather.5.cloned.1.call-start = ((), (), s32[]{:S(2)}) async-start(), calls=%async_computation.7 | async-start | bytes 106954752 | tf_op jit(solution)/shard_map/all_gather | solution.py:52
  758.8 8.2 copy-start
  767.4 64.9 %copy-start.2 = (f32[64,2048]{1,0:T(8,128)}, f32[64,2048]{1,0:T(8,128)S(1)}, u32[]{:S(2)}) copy-start(f32[64,2048]{1,0:T(8,128)S(1)} %get-tuple-element.10) | copy-start | bytes 1572868
  1507.4 8.2 copy-start.3
  1591.7 30.7 %all-to-all-start.5 = ((bf16[64,32,512]{2,0,1:T(8,128)(2,1)}), bf16[64,32,512]{2,0,1:T(8,128)(2,1)S(1)}, u32[]{:S(2)}, u32[]{:S(2)}) async-start(bf16[64,32,512]{2,0,1:T(8,128)(2,1)} %select_bitcast_fusion), calls=%async_computation.5 | async-start | bytes 4194304 | tf_op jit(solution)/shard_map/all_to_all | solution.py:30
  1603.4 27.2 %copy-start.1 = (f32[64,2048]{1,0:T(8,128)S(1)}, f32[64,2048]{1,0:T(8,128)}, u32[]{:S(2)}) copy-start(f32[64,2048]{1,0:T(8,128)} %param.8) | copy-start | bytes 1572868
Sparse Core Ops, SparseCore 0:
  133.9 536.1 all-gather.2
  878.8 535.7 all-gather.4
